TPU v7x, 128 devices: a whole 4x4x4 slice. The times are simulated.
128 devices in a mesh: chan: 32 (over y_hi, x, z), win: 4 (over y_lo, core).
Axes of the slice: x: 4, y: 4 (y_hi: 2, y_lo: 2; y = y_hi * 2 + y_lo), z: 4, core: 2. Of those that a mesh axis runs over, the one named last changes fastest.
Arguments:
- records: bfloat16 [10240, 102400], P('chan', 'win'), may hold values from -6 to 6
- offsets: int32 [32], P('win'), may hold values from 0 to 128
- src_index: int32 [4, 4], replicated, may hold values from 0 to 10239, as said below
- quality: int32 [10240], P('chan'), may hold values 0 or 1
Outputs:
- stacks: float32 [4, 196, 10240], P('win', None, 'chan')
Inputs may be any that keep to these rules, and one draw needn't show every extreme that they name: `src_index`: the 4 channels of one step are distinct and lie in one aligned block of 320 channels; some step includes channel 0 and some other step the last channel.
All inputs are finite; a program needn't handle non-finite values. No bound on the sum of `quality` on one device may be relied on, other than what follows from the above.
Results may differ from a plain program's by a relative error of at most 0.0038.
Values may be sent and summed in bfloat16 or wider, within the bound.
A program may use at most 256 MiB of HBM per device.

v0:
```python
import math

import jax
import jax.numpy as jnp
from jax import lax
from jax.sharding import PartitionSpec as P

L = 3072
LAGS = 49


EPSILON = 1e-06


def spread(value, axis, source):
    kept = jnp.where(lax.axis_index(axis) == source, value, 0).astype(value.dtype)
    return lax.psum(kept, axis)


def whiten(segment):
    values = segment.astype(jnp.float32)
    power = jnp.mean(values * values, axis=-1, keepdims=True)
    return (values / jnp.sqrt(power + EPSILON)).astype(jnp.bfloat16)


def lagged(source):
    half = (LAGS - 1) // 2
    length = source.shape[-1]
    widths = [(0, 0)] * (source.ndim - 1) + [(half, half)]
    padded = jnp.pad(source, widths)
    return jnp.stack(
        [padded[..., 2 * half - column : 2 * half - column + length] for column in range(LAGS)],
        axis=-2,
    )


def body(records, offsets, src_index, quality):
    channels = records.shape[0]
    seg_count = offsets.shape[0]
    stride = records.shape[1] // seg_count
    step_count = src_index.shape[0]
    src_count = src_index.shape[1]
    starts = jnp.arange(seg_count, dtype=jnp.int32) * stride + offsets

    def cut_segment(begin):
        return lax.dynamic_slice_in_dim(records, begin, L, 1)

    white = whiten(jax.vmap(cut_segment)(starts))
    owners = src_index[:, 0] // channels
    local_rows = src_index % channels
    received = []
    for number in range(step_count):
        candidate = jnp.take(white, local_rows[number], axis=1)
        received.append(spread(candidate, "chan", owners[number]))
    sources = jnp.stack(received)

    def step_term(source):
        shifted = lagged(source).reshape(seg_count, src_count * LAGS, L)
        return lax.dot_general(
            shifted, white, (((0, 2), (0, 2)), ((), ())), preferred_element_type=jnp.float32
        )

    terms = jnp.stack([step_term(sources[number]) for number in range(step_count)])
    summed = lax.psum_scatter(terms, "win", scatter_dimension=0, tiled=True)
    scale = 1.0 / math.sqrt(seg_count * lax.axis_size("win") * L)
    return summed * scale * quality.astype(jnp.float32)[None, None, :]


def solution(mesh):
    return jax.shard_map(
        body,
        mesh=mesh,
        in_specs=(P("chan", "win"), P("win"), P(), P("chan")),
        out_specs=P("win", None, "chan"),
        check_vma=False,
    )
```

profile of v0, /device:TPU:1, one launch (start us, length us, event | category | flops | bytes accessed | tf_op | source)
XLA Modules:
  0.0 860.5 jit_solution(8085900985988413028)
XLA Ops:
  9.5 40.1 %while.1 = (s32[]{:T(128)}, bf16[320,25600]{1,0:T(8,128)(2,1)}, s32[8,2]{0,1:T(2,128)S(1)}, bf16[8,320,3072]{2,1,0:T(8,128)(2,1)}, s32[]{:T(128)}) while((s32[]{:T(128)}, bf16[320,25600]{1,0:T(8,128)(2,1)}, s32[8,2]{0,1:T(2,128)S(1)}, bf16[8,320,3072]{2,1,0:T(8,128)(2,1)}, s32[]{:T(128)}) %tuple.32), condition=%wide.while_cond, body=%wide.while_body.sunk | while | flops 2 | bytes 3933273 | solution.py:46
  10.1 4.3 bitcast_dynamic-update-slice_fusion.2
  15.1 4.4 bitcast_dynamic-update-slice_fusion.2
  20.1 4.4 bitcast_dynamic-update-slice_fusion.2
  25.1 4.4 bitcast_dynamic-update-slice_fusion.2
  30.1 4.4 bitcast_dynamic-update-slice_fusion.2
  35.2 4.4 bitcast_dynamic-update-slice_fusion.2
  40.3 4.4 bitcast_dynamic-update-slice_fusion.2
  45.3 4.4 bitcast_dynamic-update-slice_fusion.2
  49.6 27.3 %fusion = f32[8,320]{0,1:T(8,128)S(1)} fusion(bf16[8,320,3072]{2,1,0:T(8,128)(2,1)} %get-tuple-element.13), kind=kLoop, calls=%fused_computation.8 | loop fusion | flops 23590400 | bytes 15738880 | tf_op jit(solution)/shard_map/reduce_sum | solution.py:22
  77.2 32.5 %fusion.1 = bf16[8,320,3072]{2,0,1:T(8,128)(2,1)} fusion(f32[8,320]{0,1:T(8,128)S(1)} %copy.55, bf16[8,320,3072]{2,1,0:T(8,128)(2,1)} %get-tuple-element.13), kind=kLoop, calls=%fused_computation.9 | loop fusion | flops 23592960 | bytes 31467520 | tf_op jit(solution)/shard_map/convert_element_type | solution.py:23
  109.7 6.0 gather_fusion
  115.8 6.0 gather_fusion.1
  123.8 6.0 gather_fusion.2
  129.8 6.0 gather_fusion.3
  137.2 0.9 bitcast_select_fusion.2
  138.1 0.9 bitcast_select_fusion
  139.2 334.6 %all-reduce.9.cloned.1.call-done = (bf16[8,4,3072]{2,0,1:T(8,128)(2,1)}, bf16[8,4,3072]{2,0,1:T(8,128)(2,1)}, bf16[8,4,3072]{2,0,1:T(8,128)(2,1)}, bf16[8,4,3072]{2,0,1:T(8,128)(2,1)}) async-done(((bf16[8,4,3072]{2,0,1:T(8,128)(2,1)}, bf16[8,4,3072]{2,0,1:T(8,128)(2,1)}, bf16[8,4,3072]{2,0,1:T(8,128)(2,1)}, bf16[8,4,3072]{2,0,1:T(8,128)(2,1)}), (bf16[8,4,3072]{2,0,1:T(8,128)(2,1)}, ...) | async-done | bytes 786448 | tf_op jit(solution)/shard_map/psum | solution.py:17
  473.9 1.8 constant_dynamic-update-slice_fusion.48
  475.7 1.7 constant_dynamic-update-slice_fusion.47
  477.4 1.7 constant_dynamic-update-slice_fusion.46
  479.1 1.7 constant_dynamic-update-slice_fusion.45
  480.8 1.7 constant_dynamic-update-slice_fusion.44
  482.6 1.7 constant_dynamic-update-slice_fusion.43
  484.3 1.7 constant_dynamic-update-slice_fusion.42
  486.0 1.7 constant_dynamic-update-slice_fusion.41
  487.8 1.7 constant_dynamic-update-slice_fusion.40
  489.5 1.7 constant_dynamic-update-slice_fusion.39
  491.2 1.7 constant_dynamic-update-slice_fusion.38
  492.9 1.7 constant_dynamic-update-slice_fusion.37
  494.6 1.7 constant_dynamic-update-slice_fusion.36
  496.4 1.7 constant_dynamic-update-slice_fusion.35
  498.1 1.7 constant_dynamic-update-slice_fusion.34
  499.8 1.7 constant_dynamic-update-slice_fusion.33
  501.5 1.7 constant_dynamic-update-slice_fusion.32
  503.3 1.7 constant_dynamic-update-slice_fusion.31
  505.0 1.7 constant_dynamic-update-slice_fusion.30
  506.7 1.7 constant_dynamic-update-slice_fusion.29
  508.4 1.7 constant_dynamic-update-slice_fusion.28
  510.2 1.7 constant_dynamic-update-slice_fusion.27
  511.9 1.7 constant_dynamic-update-slice_fusion.26
  513.6 1.7 constant_dynamic-update-slice_fusion.25
  515.3 1.6 constant_dynamic-update-slice_fusion.24
  528.9 0.8 constant_dynamic-update-slice_fusion.8
  534.6 0.8 constant_dynamic-update-slice_fusion.1
  536.2 8.4 copy.56
  544.6 29.6 %fusion.14 = f32[1,196,320]{2,1,0:T(8,128)S(1)} fusion(bf16[8,320,3072]{2,0,1:T(8,128)(2,1)} %fusion.1, bf16[8,196,3072]{2,0,1:T(8,128)(2,1)} %bitcast.443), kind=kOutput, calls=%fused_computation.23 | convolution fusion | flops 3082813440 | bytes 25613312 | tf_op jit(solution)/shard_map/dot_general | solution.py:59
  606.2 0.8 constant_dynamic-update-slice_fusion.57
  611.8 0.8 constant_dynamic-update-slice_fusion.50
  613.4 8.4 copy.59
  621.8 29.8 %fusion.19 = f32[1,196,320]{2,1,0:T(8,128)S(1)} fusion(bf16[8,320,3072]{2,0,1:T(8,128)(2,1)} %fusion.1, bf16[8,196,3072]{2,0,1:T(8,128)(2,1)} %bitcast.444), kind=kOutput, calls=%fused_computation.24 | convolution fusion | flops 3082813440 | bytes 25613312 | tf_op jit(solution)/shard_map/dot_general | solution.py:59
  683.5 0.8 constant_dynamic-update-slice_fusion.106
  689.1 0.8 constant_dynamic-update-slice_fusion.99
  690.8 8.4 copy.62
  699.2 29.4 %fusion.24 = f32[1,196,320]{2,1,0:T(8,128)S(1)} fusion(bf16[8,320,3072]{2,0,1:T(8,128)(2,1)} %fusion.1, bf16[8,196,3072]{2,0,1:T(8,128)(2,1)} %bitcast.445), kind=kOutput, calls=%fused_computation.25 | convolution fusion | flops 3082813440 | bytes 25613312 | tf_op jit(solution)/shard_map/dot_general | solution.py:59
  731.9 0.8 constant_dynamic-update-slice_fusion.191
  738.3 0.8 constant_dynamic-update-slice_fusion.183
  743.9 0.8 constant_dynamic-update-slice_fusion.176
  767.7 8.4 copy.65
  776.1 29.4 %fusion.29 = f32[1,196,320]{2,1,0:T(8,128)S(1)} fusion(bf16[8,320,3072]{2,0,1:T(8,128)(2,1)} %fusion.1, bf16[8,196,3072]{2,0,1:T(8,128)(2,1)} %bitcast.442), kind=kOutput, calls=%fused_computation.26 | convolution fusion | flops 3082813440 | bytes 25613312 | tf_op jit(solution)/shard_map/dot_general | solution.py:59
  805.6 1.2 pad_maximum_fusion
  806.8 44.7 %reduce-scatter.5.cloned.1.call-done = f32[1,196,320]{2,1,0:T(8,128)} async-done(((f32[4,196,320]{2,1,0:T(8,128)}), f32[1,196,320]{2,1,0:T(8,128)}) %reduce-scatter.5.cloned.1.call-update) | async-done | bytes 250896
  851.4 1.0 broadcast_multiply_fusion
  852.4 1.0 copy.68
  (209 shorter events, 138.2 us)
Async XLA Ops:
  6.5 467.3 %all-reduce.9.cloned.1.call-start = ((), (), s32[]{:S(2)}) async-start(), calls=%async_computation.2 | async-start | bytes 1572864 | tf_op jit(solution)/shard_map/psum | solution.py:17
  139.0 712.4 %reduce-scatter.5.cloned.1.call-start = ((), (), s32[]{:S(2)}) async-start(), calls=%async_computation.1 | async-start | bytes 1536000
  473.9 43.1 %copy-start.3 = (bf16[8,4,3072]{2,0,1:T(8,128)(2,1)S(1)}, bf16[8,4,3072]{2,0,1:T(8,128)(2,1)}, u32[]{:S(2)}) copy-start(bf16[8,4,3072]{2,0,1:T(8,128)(2,1)} %get-tuple-element.25) | copy-start | bytes 589828
  544.6 29.7 %copy-start.2 = (bf16[8,4,3072]{2,0,1:T(8,128)(2,1)S(1)}, bf16[8,4,3072]{2,0,1:T(8,128)(2,1)}, u32[]{:S(2)}) copy-start(bf16[8,4,3072]{2,0,1:T(8,128)(2,1)} %get-tuple-element.24) | copy-start | bytes 589828
  621.8 29.8 %copy-start.1 = (bf16[8,4,3072]{2,0,1:T(8,128)(2,1)S(1)}, bf16[8,4,3072]{2,0,1:T(8,128)(2,1)}, u32[]{:S(2)}) copy-start(bf16[8,4,3072]{2,0,1:T(8,128)(2,1)} %get-tuple-element.23) | copy-start | bytes 589828
  699.2 29.4 %copy-start = (bf16[8,4,3072]{2,0,1:T(8,128)(2,1)S(1)}, bf16[8,4,3072]{2,0,1:T(8,128)(2,1)}, u32[]{:S(2)}) copy-start(bf16[8,4,3072]{2,0,1:T(8,128)(2,1)} %get-tuple-element.22) | copy-start | bytes 589828
  776.1 30.6 %copy-start.4 = (s32[320]{0:T(512)S(1)}, s32[320]{0:T(512)}, u32[]{:S(2)}) copy-start(s32[320]{0:T(512)} %param.9) | copy-start | bytes 3844
Sparse Core Ops, SparseCore 0:
  139.1 334.6 all-reduce.8
  806.9 44.5 reduce-scatter.4
where the time goes:
time: 869 us; the launch traced here: 861 us
  waiting for transfers between devices  379 us (44%)
  local copies, waits for them, and re-layouts  279 us (32%)
  matrix products  118 us (14%)
  other arithmetic  66.8 us (8%)
  between operations  16.5 us (2%)
    psum x1, waiting for transfers between devices, spread(): return lax.psum(kept, axis)  335 us
    unnamed x202, local copies, waits for them, and re-layouts  176 us
    dot_general x4, matrix products, step_term(): lax.dot_general(shifted, white, (((0, 2), (0, 2)), ((), ())), preferred_e...  118 us
    unnamed x3, waiting for transfers between devices  44.7 us
    gather x24, local copies, waits for them, and re-layouts  40.1 us
    another operation x8, local copies, waits for them, and re-layouts, lagged(): jnp.stack([padded[..., 2 * half - column:2 * half - column + length] for...  36.9 us
    convert_element_type x1, other arithmetic, whiten(): return (values / jnp.sqrt(power + EPSILON)).astype(jnp.bfloat16)  32.5 us
    reduce_sum x1, other arithmetic, whiten(): power = jnp.mean(values * values, axis=-1, keepdims=True)  27.3 us
  transfers between devices with their start and end apart: 2, of which 2 were waited for; matrix products, arithmetic and copies ran while one was open for 0% of the time, Pallas kernels for 0%

commit v1 on v0

v1 whole, which is shorter than its diff:
```python
import functools
import math

import jax
import jax.numpy as jnp
from jax import lax
from jax.experimental import pallas as pl
from jax.experimental.pallas import tpu as pltpu
from jax.sharding import PartitionSpec as P

L = 3072
LAGS = 49
EPSILON = 1e-06
LANES = 128
PIECE = 256
EIGHT = 8
PAD = 64
MESH = pl.DeviceIdType.MESH
VMEM_BYTES = 60 << 20


class Sizes:
    def __init__(self, channels, samples, segs, steps, srcs, chans, wins):
        self.channels, self.segs, self.steps, self.srcs = channels, segs, steps, srcs
        self.chans, self.wins = chans, wins
        self.width = samples // segs
        self.tiles = self.width // LANES
        self.rows = steps * srcs
        self.piece_tiles = PIECE // LANES
        self.pieces = -(-self.tiles // self.piece_tiles)
        self.plane = chans // 2
        self.side = math.isqrt(self.plane)
        self.groups = -(-LAGS // EIGHT)
        self.zrows = self.width + 2 * PAD
        assert self.rows * EIGHT == LANES and self.side**2 == self.plane and wins == 4
        assert self.pieces == self.plane - self.side + 1


def in_segment(z, tile, value, off):
    if 0 < tile < z.tiles - 1:
        return value
    lane = lax.broadcasted_iota(jnp.int32, value.shape, 1)
    return jnp.where(lane >= off if tile == 0 else lane < off, value, 0.0)


def pick(z, records, seg, onehot, off, cand):
    rows = jnp.dot(onehot, records[seg], preferred_element_type=jnp.float32)
    tiles = [in_segment(z, t, rows[:, t * LANES : (t + 1) * LANES], off) for t in range(z.tiles)]
    power = jnp.sum(sum(value * value for value in tiles), axis=1, keepdims=True) * (1.0 / L)
    factor = 1.0 / jnp.sqrt(power + EPSILON)
    for t, value in enumerate(tiles):
        lanes = t % z.piece_tiles * LANES
        cand[seg, t // z.piece_tiles, :, lanes : lanes + LANES] = (value * factor).astype(jnp.bfloat16)
    for t in range(z.tiles, z.pieces * z.piece_tiles):
        lanes = t % z.piece_tiles * LANES
        cand[seg, t // z.piece_tiles, :, lanes : lanes + LANES] = jnp.zeros((z.rows, LANES), jnp.bfloat16)


def measure_power(z, records, seg, off, factors):
    count = 32

    @pl.loop(0, z.channels // count)
    def _(block):
        at = pl.ds(pl.multiple_of(block * count, count), count)
        total = jnp.zeros((count, LANES), jnp.float32)
        for t in range(z.tiles):
            value = in_segment(z, t, records[seg, at, t * LANES : (t + 1) * LANES].astype(jnp.float32), off)
            if t == 0 or t == z.tiles - 1:
                records[seg, at, t * LANES : (t + 1) * LANES] = value.astype(jnp.bfloat16)
            total = total + value * value
        power = jnp.sum(total, axis=1, keepdims=True) * (1.0 / L)
        factors[seg, at, :] = jnp.broadcast_to(1.0 / jnp.sqrt(power + EPSILON), (count, LANES))


def spread_lags(z, full, seg, turned):
    lane = lax.broadcasted_iota(jnp.int32, (z.rows, LANES), 1)
    zero = jnp.zeros((z.rows, LANES), jnp.bfloat16)

    def tile(t):
        if t < 0 or t >= z.tiles:
            return zero
        lanes = t % z.piece_tiles * LANES
        return full[seg, t // z.piece_tiles, :, lanes : lanes + LANES]

    before = [zero] * EIGHT
    turned[0:PAD, :] = jnp.zeros((PAD, LANES), jnp.bfloat16)
    for t in range(z.tiles + 1):
        now = tile(t)
        rolled = [now] + [pltpu.roll(now, e, 1) if t < z.tiles else zero for e in range(1, EIGHT)]
        stack = [now] + [jnp.where(lane < e, before[e], rolled[e]) for e in range(1, EIGHT)]
        block = jnp.concatenate(stack, axis=0).T
        if t < z.tiles:
            turned[PAD + t * LANES : PAD + (t + 1) * LANES, :] = block
        else:
            turned[PAD + z.width : z.zrows, :] = block[0:PAD]
        before = rolled


def correlate(z, records, seg, factors, turned, total):
    half = z.groups // 2
    for first in range(0, z.groups, 2):
        groups = range(first, min(first + 2, z.groups))
        lagged = jnp.concatenate(
            [turned[PAD - EIGHT * (a - half) : PAD - EIGHT * (a - half) + z.width, :] for a in groups], axis=1
        )
        term = lax.dot_general(records[seg], lagged, (((1,), (0,)), ((), ())), preferred_element_type=jnp.float32)
        for n, a in enumerate(groups):
            scaled = term[:, n * LANES : (n + 1) * LANES] * factors[seg]
            at = slice(a * LANES, (a + 1) * LANES)
            total[:, at] = scaled if seg == 0 else total[:, at] + scaled


def service_order(z):
    tasks, done = [], 0.0
    for seg in range(z.segs):
        at = 3.0 + 1.5 * seg
        late = (("choose", 0.0), ("power", 1.0), ("first", 3.3), ("second", 6.1), ("publish", 9.0), ("forward", 11.8))
        tasks += [(at + lag, seg, name) for name, lag in late]
        done = max(at + 15.0, done + 2.7)
        tasks.append((done, seg, "product"))
    return [(name, seg) for _, seg, name in sorted(tasks)]


def main_kernel(
    z, src_index, offsets, records_hbm, out,
    records, factors, cand, recv_first, part, recv_second, mine, other, full, turned_a, turned_b, total, flipped,
    blocks, pair_in, near_out, near_in,
    load_sem, first_send, first_recv, second_send, second_recv, y_send, y_recv, near_send, near_recv, group_send,
    group_recv, win_send, win_recv,
):
    chan, win = lax.axis_index("chan"), lax.axis_index("win")
    plane, place = chan // z.plane * z.plane, chan % z.plane
    across = (chan + z.plane) % z.chans
    core_peer = win + 1 - 2 * (win % 2)
    y_peer = (win + 2) % 4
    diagonal = (core_peer + 2) % 4
    side = z.side
    coords = (place // side, place % side)
    strides = (side, 1)
    whole_groups = z.pieces // side

    def peer(axis, step):
        at = coords[axis]
        return chan + ((at + step) % side - at) * strides[axis]

    def group_at(seg, step=0):
        return (coords[seg % 2] + step + seg // 2) % side

    def sub_at(seg, step=0):
        return (coords[1 - seg % 2] + step + seg) % side

    def is_piece(seg, step=0):
        return (group_at(seg) < whole_groups) | (sub_at(seg, step) == 0)

    def load(seg):
        return pltpu.make_async_copy(
            records_hbm.at[:, pl.ds(seg * z.width, z.width)], records.at[seg], load_sem.at[seg]
        )

    for seg in range(z.segs):
        load(seg).start()

    barrier = pltpu.get_barrier_semaphore()
    for axis in range(2):
        for step in range(1, side):
            pl.semaphore_signal(barrier, inc=1, device_id={"chan": peer(axis, step)}, device_id_type=MESH)
    pl.semaphore_signal(barrier, inc=1, device_id={"chan": across}, device_id_type=MESH)
    pl.semaphore_signal(barrier, inc=1, device_id={"win": core_peer}, device_id_type=MESH)
    pl.semaphore_signal(barrier, inc=1, device_id={"win": y_peer}, device_id_type=MESH)
    peers = 2 * (side - 1) + 3

    def remote(src, dst, send, recv, chan_to):
        return pltpu.make_async_remote_copy(
            src_ref=src, dst_ref=dst, send_sem=send, recv_sem=recv, device_id={"chan": chan_to}, device_id_type=MESH
        )

    steps = range(1, side)

    def to_group(seg, step):
        group, axis = group_at(seg, step), seg % 2
        send, recv = first_send.at[seg, step - 1], first_recv.at[seg, step - 1]
        whole = remote(
            cand.at[seg, pl.ds(group * side, side)], recv_first.at[seg, step - 1], send, recv, peer(axis, step)
        )
        single = remote(
            cand.at[seg, pl.ds(group * side, 1)], recv_first.at[seg, step - 1, pl.ds(0, 1)], send, recv,
            peer(axis, step),
        )
        return group < whole_groups, whole, single

    def to_piece(seg, step):
        copy = remote(
            part.at[seg, sub_at(seg, step)], recv_second.at[seg, step - 1], second_send.at[seg, step - 1],
            second_recv.at[seg, step - 1], peer(1 - seg % 2, step),
        )
        return is_piece(seg, step), copy

    def exchange(seg):
        return remote(mine.at[seg, 0], other.at[seg], y_send.at[seg], y_recv.at[seg], across)

    def piece_here(seg):
        return group_at(seg) * side + sub_at(seg)

    def to_line(seg, step):
        return remote(
            mine.at[seg, 1], full.at[seg, piece_here(seg)], near_send.at[seg, step - 1], near_recv.at[seg, step - 1],
            peer(1 - seg % 2, step),
        )

    def to_all(seg, step):
        send, recv, to = group_send.at[seg, step - 1], group_recv.at[seg, step - 1], peer(seg % 2, step)
        whole = full.at[seg, pl.ds(group_at(seg) * side, side)]
        single = full.at[seg, pl.ds(group_at(seg) * side, 1)]
        return remote(whole, whole, send, recv, to), remote(single, single, send, recv, to)

    def either(test, yes, no):
        pl.when(test)(yes)
        pl.when(jnp.logical_not(test))(no)

    def offer(seg):
        for step in steps:
            test, whole, single = to_group(seg, step)
            either(test, whole.start, single.start)

    def first(seg):
        def sum_pieces(count):
            for step in steps:
                to_group(seg, step)[1 if count > 1 else 2].wait_recv()
            for n in range(count):
                value = cand[seg, group_at(seg) * side + n]
                for step in steps:
                    value = value + recv_first[seg, step - 1, n]
                part[seg, n] = value

        either(group_at(seg) < whole_groups, lambda: sum_pieces(side), lambda: sum_pieces(1))
        for step in steps:
            test, copy = to_piece(seg, step)
            pl.when(test)(copy.start)

    def second(seg):
        @pl.when(is_piece(seg))
        def _():
            for step in steps:
                to_piece(seg, step)[1].wait_recv()
            value = part[seg, sub_at(seg)]
            for step in steps:
                value = value + recv_second[seg, step - 1]
            mine[seg, 0] = value
            exchange(seg).start()

    def publish(seg):
        @pl.when(is_piece(seg))
        def _():
            exchange(seg).wait_recv()
            value = mine[seg, 0] + other[seg]
            mine[seg, 1] = value
            for step in steps:
                to_line(seg, step).start()
            full[seg, piece_here(seg)] = value

    def forward(seg):
        for step in steps:
            pl.when(is_piece(seg, side - step))(to_line(seg, step).wait_recv)
        for step in steps:
            whole, single = to_all(seg, step)
            either(group_at(seg) < whole_groups, whole.start, single.start)

    def arrive(seg):
        for step in steps:
            whole, single = to_all(seg, step)
            either(group_at(seg, side - step) < whole_groups, whole.wait_recv, single.wait_recv)

    def drain(seg):
        for step in steps:
            test, whole, single = to_group(seg, step)
            either(test, whole.wait_send, single.wait_send)
            test, copy = to_piece(seg, step)
            pl.when(test)(copy.wait_send)
            whole, single = to_all(seg, step)
            either(group_at(seg) < whole_groups, whole.wait_send, single.wait_send)

        @pl.when(is_piece(seg))
        def _():
            exchange(seg).wait_send()
            for step in steps:
                to_line(seg, step).wait_send()

    row = lax.broadcasted_iota(jnp.int32, (z.rows, z.channels), 0)
    wanted_row = jnp.zeros((z.rows, z.channels), jnp.int32)
    for n in range(z.rows):
        wanted_row = jnp.where(row == n, src_index[n // z.srcs, n % z.srcs], wanted_row)
    held = lax.broadcasted_iota(jnp.int32, (z.rows, z.channels), 1) + chan * z.channels
    onehot = (held == wanted_row).astype(jnp.float32).astype(jnp.bfloat16)

    def choose(seg):
        load(seg).wait()
        pick(z, records, seg, onehot, offsets[seg], cand)

    def power(seg):
        measure_power(z, records, seg, offsets[seg], factors)

    turned = (turned_a, turned_b)

    def product(seg):
        arrive(seg)
        spread_lags(z, full, seg, turned[seg % 2])
        correlate(z, records, seg, factors, turned[seg % 2], total)

    tasks = {
        "power": power, "first": first, "second": second, "publish": publish, "forward": forward, "product": product,
    }
    for name, seg in service_order(z):
        if name == "choose":
            choose(seg)
            if seg == 0:
                pl.semaphore_wait(barrier, peers)
            offer(seg)
        else:
            tasks[name](seg)

    for at in range(0, z.channels, LANES):
        count = min(LANES, z.channels - at)
        flipped[at // LANES, :, 0:count] = total[at : at + count, :].T
        for step in range(z.steps):
            for i in range(z.srcs):
                value = flipped[at // LANES, pl.ds(step * z.srcs + i, LAGS, stride=z.rows), :]
                blocks[step, i * LAGS : (i + 1) * LAGS, at : at + count] = value[:, 0:count]

    def send(src, dst, number, peer):
        return pltpu.make_async_remote_copy(
            src_ref=src, dst_ref=dst, send_sem=win_send.at[number], recv_sem=win_recv.at[number],
            device_id={"win": peer}, device_id_type=MESH,
        )

    length = z.srcs * LAGS
    cut = length // 4 // EIGHT * EIGHT
    parts = [pl.ds(n * cut, cut if n < 3 else length - 3 * cut) for n in range(4)]
    far = [send(blocks.at[diagonal, at], pair_in.at[1, at], n, core_peer) for n, at in enumerate(parts)]
    own = [send(blocks.at[core_peer, at], pair_in.at[0, at], 4 + n, core_peer) for n, at in enumerate(parts)]
    last = [send(near_out.at[at], near_in.at[at], 8 + n, y_peer) for n, at in enumerate(parts)]
    for copy in far + own:
        copy.start()
    for n, at in enumerate(parts):
        far[n].wait_recv()
        near_out[at] = blocks[y_peer, at] + pair_in[1, at]
        last[n].start()
    for n, at in enumerate(parts):
        own[n].wait_recv()
        last[n].wait_recv()
        out[0, at] = blocks[win, at] + pair_in[0, at] + near_in[at]

    for seg in range(z.segs):
        drain(seg)
    for copy in far + own + last:
        copy.wait_send()


def body(chans, wins, records, offsets, src_index, quality):
    z = Sizes(*records.shape, offsets.shape[0], *src_index.shape, chans, wins)
    smem = pl.BlockSpec(memory_space=pltpu.SMEM)
    vmem = pl.BlockSpec(memory_space=pltpu.VMEM)
    hbm = pl.BlockSpec(memory_space=pl.ANY)
    bf16, f32 = jnp.bfloat16, jnp.float32
    dma = pltpu.SemaphoreType.DMA
    piece = (z.rows, PIECE)
    block = (z.srcs * LAGS, z.channels)
    sums = pl.pallas_call(
        functools.partial(main_kernel, z),
        out_shape=jax.ShapeDtypeStruct((1, *block), f32),
        in_specs=[smem, smem, hbm],
        out_specs=vmem,
        scratch_shapes=[
            pltpu.VMEM((z.segs, z.channels, z.width), bf16),
            pltpu.VMEM((z.segs, z.channels, LANES), f32),
            pltpu.VMEM((z.segs, z.plane, *piece), bf16),
            pltpu.VMEM((z.segs, z.side - 1, z.side, *piece), bf16),
            pltpu.VMEM((z.segs, z.side, *piece), bf16),
            pltpu.VMEM((z.segs, z.side - 1, *piece), bf16),
            pltpu.VMEM((z.segs, 2, *piece), bf16),
            pltpu.VMEM((z.segs, *piece), bf16),
            pltpu.VMEM((z.segs, z.plane, *piece), bf16),
            pltpu.VMEM((z.zrows, LANES), bf16),
            pltpu.VMEM((z.zrows, LANES), bf16),
            pltpu.VMEM((z.channels, z.groups * LANES), f32),
            pltpu.VMEM((-(-z.channels // LANES), z.groups * LANES, LANES), f32),
            pltpu.VMEM((z.steps, *block), f32),
            pltpu.VMEM((2, *block), f32),
            pltpu.VMEM(block, f32),
            pltpu.VMEM(block, f32),
            dma((z.segs,)),
            dma((z.segs, z.side - 1)),
            dma((z.segs, z.side - 1)),
            dma((z.segs, z.side - 1)),
            dma((z.segs, z.side - 1)),
            dma((z.segs,)),
            dma((z.segs,)),
            dma((z.segs, z.side - 1)),
            dma((z.segs, z.side - 1)),
            dma((z.segs, z.side - 1)),
            dma((z.segs, z.side - 1)),
            dma((12,)),
            dma((12,)),
        ],
        compiler_params=pltpu.CompilerParams(
            collective_id=0, has_side_effects=True, vmem_limit_bytes=VMEM_BYTES
        ),
        name="stack",
    )(src_index, offsets, records)
    scale = 1.0 / math.sqrt(z.segs * z.wins * L)
    return sums * scale * quality.astype(f32)[None, None, :]


def solution(mesh):
    return jax.shard_map(
        functools.partial(body, mesh.shape["chan"], mesh.shape["win"]),
        mesh=mesh,
        in_specs=(P("chan", "win"), P("win"), P(), P("chan")),
        out_specs=P("win", None, "chan"),
        check_vma=False,
    )
```

time: 869 us -> 67.5 us (0.08)
  waiting for transfers between devices: 379 us -> 0 us
  local copies, waits for them, and re-layouts: 279 us -> 1.03 us
  matrix products: 118 us -> 0 us
  other arithmetic: 66.8 us -> 1.67 us
  Pallas kernels: 0 us -> 64.6 us
  between operations: 16.5 us -> 0.01 us
    psum x1 -> x0, waiting for transfers between devices: 335 us -> none  [spread(): return lax.psum(kept, axis)]
    unnamed x202 -> x0, local copies, waits for them, and re-layouts: 176 us -> none
    dot_general x4 -> x0, matrix products: 118 us -> none  [step_term(): lax.dot_general(shifted, white, (((0, 2), (0, 2)), ((), ())), preferred_e...]
    pallas_call x0 -> x1, Pallas kernels: none -> 64.6 us  [body(): pl.pallas_call(functools.partial(main_kernel, z), out_shape=jax.ShapeDtyp...]
    gather x28 -> x0, local copies, waits for them, and re-layouts: 64.2 us -> none
    unnamed x3 -> x0, waiting for transfers between devices: 44.7 us -> none
    another operation x8 -> x0, local copies, waits for them, and re-layouts: 36.9 us -> none  [lagged(): jnp.stack([padded[..., 2 * half - column:2 * half - column + length] for...]
    convert_element_type x1 -> x0, other arithmetic: 32.5 us -> none  [whiten(): return (values / jnp.sqrt(power + EPSILON)).astype(jnp.bfloat16)]
  transfers between devices with their start and end apart: 2 -> 0, of which waited for: 2 -> 0; matrix products, arithmetic and copies ran while one was open for 0% -> 0% of each run, Pallas kernels for 0% -> 0%
where the time goes in v1:
time: 67.5 us; the launch traced here: 67.3 us
  Pallas kernels  64.6 us (96%)
  other arithmetic  1.67 us (2%)
  local copies, waits for them, and re-layouts  1.03 us (2%)
    pallas_call x1, Pallas kernels, body(): pl.pallas_call(functools.partial(main_kernel, z), out_shape=jax.ShapeDtyp...  64.6 us
    mul x2, other arithmetic, body(): return sums * scale * quality.astype(f32)[None, None, :]  1.67 us

profile of v1, /device:TPU:1, one launch (start us, length us, event | category | flops | bytes accessed | tf_op | source)
XLA Modules:
  0.0 67.3 jit_solution(6640720052124174208)
XLA Ops:
  0.0 0.7 %convert_multiply_fusion = f32[320]{0:T(512)S(1)} fusion(s32[320]{0:T(512)} %param.7), kind=kLoop, calls=%fused_computation.1 | loop fusion | flops 640 | bytes 2560 | tf_op jit(solution)/shard_map/mul | solution.py:410
  0.7 64.6 %stack.1 = f32[1,196,320]{2,1,0:T(8,128)} custom-call(s32[4,4]{1,0:T(4,128)} %src_index.1, s32[8]{0:T(128)} %offsets.1, bf16[320,25600]{1,0:T(8,128)(2,1)} %records_hbm.1), custom_call_target="tpu_custom_call" | custom-call | tf_op jit(solution)/shard_map/stack/pallas_call | solution.py:367
  65.3 1.0 %broadcast_multiply_fusion = f32[1,196,320]{2,1,0:T(8,128)S(1)} fusion(f32[1,196,320]{2,1,0:T(8,128)} %stack.1, f32[320]{0:T(512)S(1)} %convert_multiply_fusion), kind=kLoop, calls=%fused_computation | loop fusion | flops 62720 | bytes 503040 | tf_op jit(solution)/shard_map/mul | solution.py:410
  66.3 1.0 %copy.5 = f32[1,196,320]{2,0,1:T(1,128)} copy(f32[1,196,320]{2,1,0:T(8,128)S(1)} %broadcast_multiply_fusion) | data formatting | bytes 501760 | tf_op jit(solution)/shard_map/mul | solution.py:410

commit v2 on v1

v2 whole, which is shorter than its diff:
```python
import functools
import math

import jax
import jax.numpy as jnp
from jax import lax
from jax.experimental import pallas as pl
from jax.experimental.pallas import tpu as pltpu
from jax.sharding import PartitionSpec as P

L = 3072
LAGS = 49
EPSILON = 1e-06
LANES = 128
FIRST_PART = 192
EIGHT = 8
PAD = 64
MESH = pl.DeviceIdType.MESH
VMEM_BYTES = 60 << 20


class Sizes:
    def __init__(self, channels, samples, segs, steps, srcs, chans, wins):
        self.channels, self.segs, self.steps, self.srcs = channels, segs, steps, srcs
        self.chans, self.wins = chans, wins
        self.width = samples // segs
        self.tiles = self.width // LANES
        self.rows = steps * srcs
        self.plane = chans // 2
        self.side = math.isqrt(self.plane)
        self.pair = 2 * self.side
        self.slots = self.side * self.pair
        self.whole_groups = self.tiles // self.pair
        self.groups = -(-LAGS // EIGHT)
        self.zrows = self.width + 2 * PAD
        assert self.rows * EIGHT == LANES and self.side**2 == self.plane and wins == 4
        assert self.tiles == self.whole_groups * self.pair + 1 and self.whole_groups == self.side - 1


def in_segment(z, tile, value, off):
    if 0 < tile < z.tiles - 1:
        return value
    lane = lax.broadcasted_iota(jnp.int32, value.shape, 1)
    return jnp.where(lane >= off if tile == 0 else lane < off, value, 0.0)


def pick(z, records, seg, onehot, off, cand):
    rows = jnp.dot(onehot, records[seg], preferred_element_type=jnp.float32)
    tiles = [in_segment(z, t, rows[:, t * LANES : (t + 1) * LANES], off) for t in range(z.tiles)]
    power = jnp.sum(sum(value * value for value in tiles), axis=1, keepdims=True) * (1.0 / L)
    factor = 1.0 / jnp.sqrt(power + EPSILON)
    for t, value in enumerate(tiles):
        cand[seg, t] = (value * factor).astype(jnp.bfloat16)


def measure_power(z, records, seg, off, factors):
    count = 32

    @pl.loop(0, z.channels // count)
    def _(block):
        at = pl.ds(pl.multiple_of(block * count, count), count)
        total = jnp.zeros((count, LANES), jnp.float32)
        for t in range(z.tiles):
            value = in_segment(z, t, records[seg, at, t * LANES : (t + 1) * LANES].astype(jnp.float32), off)
            if t == 0 or t == z.tiles - 1:
                records[seg, at, t * LANES : (t + 1) * LANES] = value.astype(jnp.bfloat16)
            total = total + value * value
        power = jnp.sum(total, axis=1, keepdims=True) * (1.0 / L)
        factors[seg, at, :] = jnp.broadcast_to(1.0 / jnp.sqrt(power + EPSILON), (count, LANES))


def spread_lags(z, full, seg, turned):
    lane = lax.broadcasted_iota(jnp.int32, (z.rows, LANES), 1)
    zero = jnp.zeros((z.rows, LANES), jnp.bfloat16)

    def tile(t):
        return full[seg, t] if t < z.tiles else zero

    before = [zero] * EIGHT
    turned[seg, 0:PAD, :] = jnp.zeros((PAD, LANES), jnp.bfloat16)
    for t in range(z.tiles + 1):
        now = tile(t)
        rolled = [now] + [pltpu.roll(now, e, 1) if t < z.tiles else zero for e in range(1, EIGHT)]
        stack = [now] + [jnp.where(lane < e, before[e], rolled[e]) for e in range(1, EIGHT)]
        block = jnp.concatenate(stack, axis=0).T
        if t < z.tiles:
            turned[seg, PAD + t * LANES : PAD + (t + 1) * LANES, :] = block
        else:
            turned[seg, PAD + z.width : z.zrows, :] = block[0:PAD]
        before = rolled


def correlate(z, records, seg, rows, factors, turned, total):
    half = z.groups // 2
    for first in range(0, z.groups, 2):
        groups = range(first, min(first + 2, z.groups))
        starts = [PAD - EIGHT * (a - half) for a in groups]
        lagged = jnp.concatenate([turned[seg, at : at + z.width, :] for at in starts], axis=1)
        term = jnp.dot(records[seg, rows, :], lagged, preferred_element_type=jnp.float32)
        for n, a in enumerate(groups):
            scaled = term[:, n * LANES : (n + 1) * LANES] * factors[seg, rows, :]
            at = slice(a * LANES, (a + 1) * LANES)
            total[rows, at] = scaled if seg == 0 else total[rows, at] + scaled


def service_order(z):
    tasks, done = [], 0.0
    for seg in range(z.segs):
        at = 3.0 + 1.3 * seg
        late = (("choose", 0.0), ("power", 1.5), ("first", 4.3), ("second", 8.4), ("forward", 12.5))
        tasks += [(at + lag, seg, name) for name, lag in late]
        done = max(at + 16.6, done + 1.5)
        tasks.append((done, seg, "product"))
    return [(name, seg) for _, seg, name in sorted(tasks)]


def main_kernel(
    z, src_index, offsets, records_hbm, out,
    records, factors, cand, recv_first, part, recv_second, mine, full, turned, total, flipped,
    blocks_a, pair_a, near_out_a, near_in_a, blocks_b, pair_b, near_out_b, near_in_b,
    load_sem, first_send, first_recv, second_send, second_recv, line_send, line_recv, group_send, group_recv,
    win_send, win_recv,
):
    chan, win = lax.axis_index("chan"), lax.axis_index("win")
    place = chan % z.plane
    level = chan // z.plane
    core_peer = win + 1 - 2 * (win % 2)
    y_peer = (win + 2) % 4
    diagonal = (core_peer + 2) % 4
    side = z.side
    coords = (place // side, place % side)
    strides = (side, 1)
    whole_groups = z.whole_groups

    def peer(axis, step, up=0):
        at = coords[axis]
        return (chan + ((at + step) % side - at) * strides[axis] + up * z.plane) % z.chans

    def group_at(seg, step=0):
        return (coords[seg % 2] + step + seg // 2) % side

    def slot_at(seg, step=0, up=0):
        return (coords[1 - seg % 2] + step + seg) % side * 2 + (level + up) % 2

    def kept(seg, step=0, up=0):
        return (group_at(seg) < whole_groups) | (slot_at(seg, step, up) == 0)

    def load(seg):
        return pltpu.make_async_copy(
            records_hbm.at[:, pl.ds(seg * z.width, z.width)], records.at[seg], load_sem.at[seg]
        )

    for seg in range(z.segs):
        load(seg).start()

    barrier = pltpu.get_barrier_semaphore()
    for axis in range(2):
        for step in range(1, side):
            pl.semaphore_signal(barrier, inc=1, device_id={"chan": peer(axis, step)}, device_id_type=MESH)
            pl.semaphore_signal(barrier, inc=1, device_id={"chan": peer(axis, step, 1)}, device_id_type=MESH)
    pl.semaphore_signal(barrier, inc=1, device_id={"chan": peer(0, 0, 1)}, device_id_type=MESH)
    pl.semaphore_signal(barrier, inc=1, device_id={"win": core_peer}, device_id_type=MESH)
    pl.semaphore_signal(barrier, inc=1, device_id={"win": y_peer}, device_id_type=MESH)
    peers = 4 * (side - 1) + 3

    def remote(src, dst, send, recv, chan_to):
        return pltpu.make_async_remote_copy(
            src_ref=src, dst_ref=dst, send_sem=send, recv_sem=recv, device_id={"chan": chan_to}, device_id_type=MESH
        )

    steps = range(1, side)
    moves = [(step, up) for step in range(side) for up in range(2)][1:]

    def to_group(seg, step):
        group, to = group_at(seg, step), peer(seg % 2, step)
        send, recv = first_send.at[seg, step - 1], first_recv.at[seg, step - 1]
        whole = remote(cand.at[seg, pl.ds(group * z.pair, z.pair)], recv_first.at[seg, step - 1], send, recv, to)
        single = remote(
            cand.at[seg, pl.ds(group * z.pair, 1)], recv_first.at[seg, step - 1, pl.ds(0, 1)], send, recv, to
        )
        return group < whole_groups, whole, single

    def to_slot(seg, n):
        step, up = moves[n]
        return kept(seg, step, up), remote(
            part.at[seg, slot_at(seg, step, up)], recv_second.at[seg, n], second_send.at[seg, n],
            second_recv.at[seg, n], peer(1 - seg % 2, step, up),
        )

    def tile_here(seg):
        return group_at(seg) * z.pair + slot_at(seg)

    def to_line(seg, n):
        return remote(
            mine.at[seg], full.at[seg, tile_here(seg)], line_send.at[seg, n], line_recv.at[seg, n],
            peer(1 - seg % 2, *moves[n]),
        )

    def to_all(seg, step):
        send, recv, to = group_send.at[seg, step - 1], group_recv.at[seg, step - 1], peer(seg % 2, step)
        whole = full.at[seg, pl.ds(group_at(seg) * z.pair, z.pair)]
        single = full.at[seg, pl.ds(group_at(seg) * z.pair, 1)]
        return remote(whole, whole, send, recv, to), remote(single, single, send, recv, to)

    def either(test, yes, no):
        pl.when(test)(yes)
        pl.when(jnp.logical_not(test))(no)

    def offer(seg):
        for step in steps:
            test, whole, single = to_group(seg, step)
            either(test, whole.start, single.start)

    def first(seg):
        def sum_tiles(count):
            for step in steps:
                to_group(seg, step)[1 if count > 1 else 2].wait_recv()
            for n in range(count):
                value = cand[seg, group_at(seg) * z.pair + n]
                for step in steps:
                    value = value + recv_first[seg, step - 1, n]
                part[seg, n] = value

        either(group_at(seg) < whole_groups, lambda: sum_tiles(z.pair), lambda: sum_tiles(1))
        for n in range(len(moves)):
            test, copy = to_slot(seg, n)
            pl.when(test)(copy.start)

    def second(seg):
        @pl.when(kept(seg))
        def _():
            for n in range(len(moves)):
                to_slot(seg, n)[1].wait_recv()
            value = part[seg, slot_at(seg)]
            for n in range(len(moves)):
                value = value + recv_second[seg, n]
            mine[seg] = value
            for n in range(len(moves)):
                to_line(seg, n).start()
            full[seg, tile_here(seg)] = value

    def forward(seg):
        for n, (step, up) in enumerate(moves):
            pl.when(kept(seg, side - step, up))(to_line(seg, n).wait_recv)
        for step in steps:
            whole, single = to_all(seg, step)
            either(group_at(seg) < whole_groups, whole.start, single.start)

    def arrive(seg):
        for step in steps:
            whole, single = to_all(seg, step)
            either(group_at(seg, side - step) < whole_groups, whole.wait_recv, single.wait_recv)

    def drain(seg):
        for step in steps:
            test, whole, single = to_group(seg, step)
            either(test, whole.wait_send, single.wait_send)
            whole, single = to_all(seg, step)
            either(group_at(seg) < whole_groups, whole.wait_send, single.wait_send)
        for n in range(len(moves)):
            test, copy = to_slot(seg, n)
            pl.when(test)(copy.wait_send)

        @pl.when(kept(seg))
        def _():
            for n in range(len(moves)):
                to_line(seg, n).wait_send()

    row = lax.broadcasted_iota(jnp.int32, (z.rows, z.channels), 0)
    wanted_row = jnp.zeros((z.rows, z.channels), jnp.int32)
    for n in range(z.rows):
        wanted_row = jnp.where(row == n, src_index[n // z.srcs, n % z.srcs], wanted_row)
    held = lax.broadcasted_iota(jnp.int32, (z.rows, z.channels), 1) + chan * z.channels
    onehot = (held == wanted_row).astype(jnp.float32).astype(jnp.bfloat16)

    def choose(seg):
        load(seg).wait()
        pick(z, records, seg, onehot, offsets[seg], cand)

    def power(seg):
        measure_power(z, records, seg, offsets[seg], factors)

    rows_a, rows_b = slice(0, FIRST_PART), slice(FIRST_PART, z.channels)

    def product(seg):
        arrive(seg)
        spread_lags(z, full, seg, turned)
        correlate(z, records, seg, rows_a, factors, turned, total)

    tasks = {"power": power, "first": first, "second": second, "forward": forward, "product": product}
    for name, seg in service_order(z):
        if name == "choose":
            choose(seg)
            if seg == 0:
                pl.semaphore_wait(barrier, peers)
            offer(seg)
        else:
            tasks[name](seg)

    def flip(rows, blocks):
        for at in range(rows.start, rows.stop, LANES):
            count, to = min(LANES, rows.stop - at), at - rows.start
            flipped[:, 0:count] = total[at : at + count, :].T
            for step in range(z.steps):
                for i in range(z.srcs):
                    value = flipped[pl.ds(step * z.srcs + i, LAGS, stride=z.rows), :]
                    blocks[step, i * LAGS : (i + 1) * LAGS, to : to + count] = value[:, 0:count]

    def send(src, dst, number, to):
        return pltpu.make_async_remote_copy(
            src_ref=src, dst_ref=dst, send_sem=win_send.at[number], recv_sem=win_recv.at[number],
            device_id={"win": to}, device_id_type=MESH,
        )

    def sum_over_win(number, blocks, pair_in, near_out, near_in):
        far = send(blocks.at[diagonal], pair_in.at[1], number, core_peer)
        own = send(blocks.at[core_peer], pair_in.at[0], number + 1, core_peer)
        last = send(near_out, near_in, number + 2, y_peer)

        def begin():
            far.start()
            own.start()

        def turn():
            far.wait_recv()
            near_out[...] = blocks[y_peer] + pair_in[1]
            last.start()

        def end():
            own.wait_recv()
            last.wait_recv()
            return blocks[win] + pair_in[0] + near_in[...]

        return begin, turn, end, (far, own, last)

    begin_a, turn_a, end_a, copies_a = sum_over_win(0, blocks_a, pair_a, near_out_a, near_in_a)
    begin_b, turn_b, end_b, copies_b = sum_over_win(3, blocks_b, pair_b, near_out_b, near_in_b)
    flip(rows_a, blocks_a)
    begin_a()
    for seg in range(z.segs):
        if seg == z.segs // 2:
            turn_a()
        correlate(z, records, seg, rows_b, factors, turned, total)
    flip(rows_b, blocks_b)
    begin_b()
    for seg in range(z.segs):
        drain(seg)
    out[0, :, rows_a] = end_a()
    turn_b()
    out[0, :, rows_b] = end_b()
    for copy in copies_a + copies_b:
        copy.wait_send()


def body(chans, wins, records, offsets, src_index, quality):
    z = Sizes(*records.shape, offsets.shape[0], *src_index.shape, chans, wins)
    smem = pl.BlockSpec(memory_space=pltpu.SMEM)
    vmem = pl.BlockSpec(memory_space=pltpu.VMEM)
    hbm = pl.BlockSpec(memory_space=pl.ANY)
    bf16, f32 = jnp.bfloat16, jnp.float32
    dma = pltpu.SemaphoreType.DMA
    tile = (z.rows, LANES)
    block = (z.srcs * LAGS, z.channels)
    moves = 2 * z.side - 1
    shares = []
    for width in (FIRST_PART, z.channels - FIRST_PART):
        share = (block[0], width)
        shares += [pltpu.VMEM(lead + share, f32) for lead in ((z.steps,), (2,), (), ())]
    sums = pl.pallas_call(
        functools.partial(main_kernel, z),
        out_shape=jax.ShapeDtypeStruct((1, *block), f32),
        in_specs=[smem, smem, hbm],
        out_specs=vmem,
        scratch_shapes=[
            pltpu.VMEM((z.segs, z.channels, z.width), bf16),
            pltpu.VMEM((z.segs, z.channels, LANES), f32),
            pltpu.VMEM((z.segs, z.slots, *tile), bf16),
            pltpu.VMEM((z.segs, z.side - 1, z.pair, *tile), bf16),
            pltpu.VMEM((z.segs, z.pair, *tile), bf16),
            pltpu.VMEM((z.segs, moves, *tile), bf16),
            pltpu.VMEM((z.segs, *tile), bf16),
            pltpu.VMEM((z.segs, z.slots, *tile), bf16),
            pltpu.VMEM((z.segs, z.zrows, LANES), bf16),
            pltpu.VMEM((z.channels, z.groups * LANES), f32),
            pltpu.VMEM((z.groups * LANES, LANES), f32),
            *shares,
            dma((z.segs,)),
            dma((z.segs, z.side - 1)),
            dma((z.segs, z.side - 1)),
            dma((z.segs, moves)),
            dma((z.segs, moves)),
            dma((z.segs, moves)),
            dma((z.segs, moves)),
            dma((z.segs, z.side - 1)),
            dma((z.segs, z.side - 1)),
            dma((6,)),
            dma((6,)),
        ],
        compiler_params=pltpu.CompilerParams(
            collective_id=0, has_side_effects=True, vmem_limit_bytes=VMEM_BYTES
        ),
        name="stack",
    )(src_index, offsets, records)
    scale = 1.0 / math.sqrt(z.segs * z.wins * L)
    return sums * scale * quality.astype(f32)[None, None, :]


def solution(mesh):
    return jax.shard_map(
        functools.partial(body, mesh.shape["chan"], mesh.shape["win"]),
        mesh=mesh,
        in_specs=(P("chan", "win"), P("win"), P(), P("chan")),
        out_specs=P("win", None, "chan"),
        check_vma=False,
    )
```

time: 67.5 us -> 65.5 us (0.970)
  Pallas kernels: 64.6 us -> 62.6 us
    pallas_call x1, Pallas kernels: 64.6 us -> 62.6 us  [body(): pl.pallas_call(functools.partial(main_kernel, z), out_shape=jax.ShapeDtyp...]
where the time goes in v2:
time: 65.5 us; the launch traced here: 65.3 us
  Pallas kernels  62.6 us (96%)
  other arithmetic  1.67 us (3%)
  local copies, waits for them, and re-layouts  1.03 us (2%)
    pallas_call x1, Pallas kernels, body(): pl.pallas_call(functools.partial(main_kernel, z), out_shape=jax.ShapeDtyp...  62.6 us
    mul x2, other arithmetic, body(): return sums * scale * quality.astype(f32)[None, None, :]  1.67 us

profile of v2, /device:TPU:1, one launch (start us, length us, event | category | flops | bytes accessed | tf_op | source)
XLA Modules:
  0.0 65.3 jit_solution(14221573486799992347)
XLA Ops:
  0.0 0.7 %convert_multiply_fusion = f32[320]{0:T(512)S(1)} fusion(s32[320]{0:T(512)} %param.7), kind=kLoop, calls=%fused_computation.1 | loop fusion | flops 640 | bytes 2560 | tf_op jit(solution)/shard_map/mul | solution.py:405
  0.7 62.6 %stack.1 = f32[1,196,320]{2,1,0:T(8,128)} custom-call(s32[4,4]{1,0:T(4,128)} %src_index.1, s32[8]{0:T(128)} %offsets.1, bf16[320,25600]{1,0:T(8,128)(2,1)} %records_hbm.1), custom_call_target="tpu_custom_call" | custom-call | tf_op jit(solution)/shard_map/stack/pallas_call | solution.py:369
  63.3 1.0 %broadcast_multiply_fusion = f32[1,196,320]{2,1,0:T(8,128)S(1)} fusion(f32[1,196,320]{2,1,0:T(8,128)} %stack.1, f32[320]{0:T(512)S(1)} %convert_multiply_fusion), kind=kLoop, calls=%fused_computation | loop fusion | flops 62720 | bytes 503040 | tf_op jit(solution)/shard_map/mul | solution.py:405
  64.3 1.0 %copy.5 = f32[1,196,320]{2,0,1:T(1,128)} copy(f32[1,196,320]{2,1,0:T(8,128)S(1)} %broadcast_multiply_fusion) | data formatting | bytes 501760 | tf_op jit(solution)/shard_map/mul | solution.py:405

commit v3 on v2

--- a/solution.py
+++ b/solution.py
@@ -107,9 +107,9 @@
     tasks, done = [], 0.0
     for seg in range(z.segs):
         at = 3.0 + 1.3 * seg
-        late = (("choose", 0.0), ("power", 1.5), ("first", 4.3), ("second", 8.4), ("forward", 12.5))
+        late = (("choose", 0.0), ("power", 2.5), ("first", 5.0), ("second", 10.2), ("forward", 15.4))
         tasks += [(at + lag, seg, name) for name, lag in late]
-        done = max(at + 16.6, done + 1.5)
+        done = max(at + 20.4, done + 1.5)
         tasks.append((done, seg, "product"))
     return [(name, seg) for _, seg, name in sorted(tasks)]
 
@@ -323,13 +323,13 @@
 
         def turn():
             far.wait_recv()
-            near_out[...] = blocks[y_peer] + pair_in[1]
+            near_out[...] = (blocks[y_peer] + pair_in[1]).astype(near_out.dtype)
             last.start()
 
         def end():
             own.wait_recv()
             last.wait_recv()
-            return blocks[win] + pair_in[0] + near_in[...]
+            return blocks[win] + pair_in[0] + near_in[...].astype(jnp.float32)
 
         return begin, turn, end, (far, own, last)
 
@@ -365,7 +365,8 @@
     shares = []
     for width in (FIRST_PART, z.channels - FIRST_PART):
         share = (block[0], width)
-        shares += [pltpu.VMEM(lead + share, f32) for lead in ((z.steps,), (2,), (), ())]
+        shares += [pltpu.VMEM((z.steps, *share), f32), pltpu.VMEM((2, *share), f32)]
+        shares += [pltpu.VMEM(share, bf16)] * 2
     sums = pl.pallas_call(
         functools.partial(main_kernel, z),
         out_shape=jax.ShapeDtypeStruct((1, *block), f32),

time: 65.5 us -> 64.4 us (0.983)
  Pallas kernels: 62.6 us -> 61.5 us
    pallas_call x1, Pallas kernels: 62.6 us -> 61.5 us  [body(): pl.pallas_call(functools.partial(main_kernel, z), out_shape=jax.ShapeDtyp...]
where the time goes in v3:
time: 64.4 us; the launch traced here: 64.2 us
  Pallas kernels  61.5 us (95%)
  other arithmetic  1.67 us (3%)
  local copies, waits for them, and re-layouts  1.03 us (2%)
    pallas_call x1, Pallas kernels, body(): pl.pallas_call(functools.partial(main_kernel, z), out_shape=jax.ShapeDtyp...  61.5 us
    mul x2, other arithmetic, body(): return sums * scale * quality.astype(f32)[None, None, :]  1.67 us

profile of v3, /device:TPU:1, one launch (start us, length us, event | category | flops | bytes accessed | tf_op | source)
XLA Modules:
  0.0 64.2 jit_solution(316845159524156856)
XLA Ops:
  0.0 0.7 %convert_multiply_fusion = f32[320]{0:T(512)S(1)} fusion(s32[320]{0:T(512)} %param.7), kind=kLoop, calls=%fused_computation.1 | loop fusion | flops 640 | bytes 2560 | tf_op jit(solution)/shard_map/mul | solution.py:406
  0.7 61.5 %stack.1 = f32[1,196,320]{2,1,0:T(8,128)} custom-call(s32[4,4]{1,0:T(4,128)} %src_index.1, s32[8]{0:T(128)} %offsets.1, bf16[320,25600]{1,0:T(8,128)(2,1)} %records_hbm.1), custom_call_target="tpu_custom_call" | custom-call | tf_op jit(solution)/shard_map/stack/pallas_call | solution.py:370
  62.2 1.0 %broadcast_multiply_fusion = f32[1,196,320]{2,1,0:T(8,128)S(1)} fusion(f32[1,196,320]{2,1,0:T(8,128)} %stack.1, f32[320]{0:T(512)S(1)} %convert_multiply_fusion), kind=kLoop, calls=%fused_computation | loop fusion | flops 62720 | bytes 503040 | tf_op jit(solution)/shard_map/mul | solution.py:406
  63.1 1.0 %copy.5 = f32[1,196,320]{2,0,1:T(1,128)} copy(f32[1,196,320]{2,1,0:T(8,128)S(1)} %broadcast_multiply_fusion) | data formatting | bytes 501760 | tf_op jit(solution)/shard_map/mul | solution.py:406
